TPU v7x, 32 devices: a whole 2x2x4 slice. The times are simulated.
32 devices in a mesh: grp: 16 (over z, x, core), uly: 2 (over y).
Axes of the slice: x: 2, y: 2, z: 4, core: 2. Of those that a mesh axis runs over, the one named last changes fastest.
Arguments:
- queries: bfloat16 [4096, 32, 128], P(('grp', 'uly')), may hold values from -16 to 16
- keys: bfloat16 [4096, 4, 128], P(('grp', 'uly')), may hold values from -8 to 8
- values: bfloat16 [4096, 4, 128], P(('grp', 'uly')), may hold values from -6 to 6
- output_cotangent: bfloat16 [4096, 32, 128], P(('grp', 'uly')), may hold values from -6 to 6
- block_lists: int32 [128, 1], replicated, may hold values from 0 to 127, as said below
- list_counts: int32 [128], replicated, may hold values from 0 to 1, as said below
Outputs:
- attended: bfloat16 [4096, 32, 128], P(('grp', 'uly'))
- query_grad: bfloat16 [4096, 32, 128], P(('grp', 'uly'))
- key_gradient: bfloat16 [4096, 4, 128], P(('grp', 'uly'))
- value_gradient: bfloat16 [4096, 4, 128], P(('grp', 'uly'))
Inputs may be any that keep to these rules, and one draw needn't show every extreme that they name: `block_lists`: calling an aligned run of 8 blocks a group: every entry of block b's list is a block of another group than b's, and the entries of all lists of one group, counted or not, lie in pairwise different groups. `list_counts`: some block counts all 1 entries in every draw.
All inputs are finite; a program needn't handle non-finite values.
Results may differ from a plain program's by a relative error of at most 0.039.
Values may be sent and summed in bfloat16 or wider, within the bound.
No kernel may reach another device: no remote copies, remote signals or barrier semaphores. Data moves between devices by JAX's collectives and lax.ppermute only.
A program may use at most 128 MiB of HBM per device.

v0:
```python
import jax
import jax.numpy as jnp
from jax import lax
from jax.sharding import PartitionSpec as P


def on_device(queries, keys, values, output_cotangent, block_lists, list_counts):
    uly_count = lax.axis_size("uly")
    grp_count = lax.axis_size("grp")
    my_group = lax.axis_index("grp")
    tokens, head_count, head_width = queries.shape
    kv_heads = keys.shape[1]
    copies = max(1, uly_count // kv_heads)
    blocks_all, remote = block_lists.shape
    per_group = blocks_all // grp_count
    block_tok = tokens * uly_count // per_group
    group_tok = tokens * uly_count
    score_scale = head_width ** (-0.5)
    lists = block_lists.reshape(grp_count, per_group, remote)
    counted = (jnp.arange(remote)[None, :] < list_counts[:, None]).reshape(
        grp_count, per_group, remote
    )
    wanted = (lists // per_group == my_group) & counted
    send_place = jnp.sum(jnp.where(wanted, lists % per_group, 0), axis=(1, 2))
    sending = jnp.any(wanted, axis=(1, 2))
    mine_source = lax.dynamic_index_in_dim(lists, my_group, 0, keepdims=False) // per_group
    mine_counted = lax.dynamic_index_in_dim(counted, my_group, 0, keepdims=False)
    trip_count = jnp.max(jnp.sum(mine_counted.astype(jnp.int32), axis=1))

    def to_blocks(array_in):
        return array_in.reshape((per_group, block_tok) + array_in.shape[1:])

    keys_wide = jnp.repeat(keys, copies, axis=1)
    values_wide = jnp.repeat(values, copies, axis=1)
    query_heads, grad_heads, key_heads, value_heads = (
        lax.all_to_all(queries, "uly", split_axis=1, concat_axis=0, tiled=True),
        lax.all_to_all(output_cotangent, "uly", split_axis=1, concat_axis=0, tiled=True),
        lax.all_to_all(keys_wide, "uly", split_axis=1, concat_axis=0, tiled=True),
        lax.all_to_all(values_wide, "uly", split_axis=1, concat_axis=0, tiled=True),
    )
    stacked = jnp.stack([to_blocks(key_heads), to_blocks(value_heads)])
    outgoing = jnp.take(stacked, send_place, axis=1)
    arrived = lax.all_to_all(outgoing, "grp", split_axis=1, concat_axis=1, tiled=True)
    kv_local = key_heads.shape[1]
    heads_local = query_heads.shape[1]
    heads_per_group = heads_local // kv_local
    query_blk = query_heads.reshape(per_group, block_tok, kv_local, heads_per_group, head_width)
    grad_blk = grad_heads.reshape(per_group, block_tok, kv_local, heads_per_group, head_width)
    key_blk = to_blocks(key_heads)
    value_blk = to_blocks(value_heads)
    far_keys = arrived[0]
    far_values = arrived[1]
    causal = jnp.arange(block_tok)[:, None] >= jnp.arange(block_tok)[None, :]

    def logits(key_rows):
        return (
            jnp.einsum("pqkgd,pjkd->pkgqj", query_blk, key_rows, preferred_element_type=jnp.float32)
            * score_scale
        )

    def slot_rows(slot_index):
        source = lax.dynamic_index_in_dim(mine_source, slot_index, 1, keepdims=False)
        counted_slot = lax.dynamic_index_in_dim(mine_counted, slot_index, 1, keepdims=False)
        return (
            jnp.take(far_keys, source, axis=0),
            jnp.take(far_values, source, axis=0),
            counted_slot,
            source,
        )

    def masked(scores, counted_slot):
        return jnp.where(counted_slot[:, None, None, None, None], scores, -jnp.inf)

    near_scores = jnp.where(causal, logits(key_blk), -jnp.inf)
    highest = jnp.max(near_scores, axis=-1)
    denominator = jnp.sum(jnp.exp(near_scores - highest[..., None]), axis=-1)

    def max_sweep(slot_index, state_pair):
        highest, denominator = state_pair
        key_rows, value_rows, counted_slot, source = slot_rows(slot_index)
        scores = masked(logits(key_rows), counted_slot)
        new_highest = jnp.maximum(highest, jnp.max(scores, axis=-1))
        denominator = denominator * jnp.exp(highest - new_highest) + jnp.sum(
            jnp.exp(scores - new_highest[..., None]), axis=-1
        )
        return (new_highest, denominator)

    highest, denominator = lax.fori_loop(0, trip_count, max_sweep, (highest, denominator))
    log_total = highest + jnp.log(denominator)

    def softmax_weights(scores):
        return jnp.exp(scores - log_total[..., None])

    summed = jnp.einsum(
        "pkgqj,pjkd->pqkgd",
        softmax_weights(near_scores).astype(jnp.bfloat16),
        value_blk,
        preferred_element_type=jnp.float32,
    )

    def value_sweep(slot_index, summed):
        key_rows, value_rows, counted_slot, source = slot_rows(slot_index)
        weights = softmax_weights(masked(logits(key_rows), counted_slot)).astype(jnp.bfloat16)
        return summed + jnp.einsum(
            "pkgqj,pjkd->pqkgd", weights, value_rows, preferred_element_type=jnp.float32
        )

    summed = lax.fori_loop(0, trip_count, value_sweep, summed)
    attended_blk = summed.astype(jnp.bfloat16)
    row_delta = jnp.transpose(
        jnp.sum(grad_blk.astype(jnp.float32) * attended_blk.astype(jnp.float32), axis=-1),
        (0, 2, 3, 1),
    )

    def backward(scores, key_rows, value_rows):
        probs = softmax_weights(scores)
        weights = probs.astype(jnp.bfloat16)
        dprobs = jnp.einsum(
            "pqkgd,pjkd->pkgqj", grad_blk, value_rows, preferred_element_type=jnp.float32
        )
        dscores = (probs * (dprobs - row_delta[..., None])).astype(jnp.bfloat16)
        query_term = jnp.einsum(
            "pkgqj,pjkd->pqkgd", dscores, key_rows, preferred_element_type=jnp.float32
        )
        key_term = (
            jnp.einsum("pkgqj,pqkgd->pjkd", dscores, query_blk, preferred_element_type=jnp.float32)
            * score_scale
        )
        value_term = jnp.einsum(
            "pkgqj,pqkgd->pjkd", weights, grad_blk, preferred_element_type=jnp.float32
        )
        return (query_term, key_term, value_term)

    query_sum, key_near, value_near = backward(near_scores, key_blk, value_blk)
    far_grads = jnp.zeros((2, grp_count, block_tok, kv_local, head_width), jnp.float32)

    def grad_sweep(slot_index, state_pair):
        query_sum, far_grads = state_pair
        key_rows, value_rows, counted_slot, source = slot_rows(slot_index)
        query_term, key_term, value_term = backward(
            masked(logits(key_rows), counted_slot), key_rows, value_rows
        )
        routing = (
            (source[:, None] == jnp.arange(grp_count)[None, :]) & counted_slot[:, None]
        ).astype(jnp.float32)
        routed = jnp.einsum(
            "ps,xpjkd->xsjkd",
            routing,
            jnp.stack([key_term, value_term]),
            precision=lax.Precision.HIGHEST,
        )
        return (query_sum + query_term, far_grads + routed)

    query_sum, far_grads = lax.fori_loop(0, trip_count, grad_sweep, (query_sum, far_grads))
    owners = ((send_place[:, None] == jnp.arange(per_group)[None, :]) & sending[:, None]).astype(
        jnp.float32
    )
    returned = lax.all_to_all(far_grads, "grp", split_axis=1, concat_axis=1, tiled=True)
    landed = jnp.einsum("sp,xsjkd->xpjkd", owners, returned, precision=lax.Precision.HIGHEST)
    key_local = (key_near + landed[0]).reshape(group_tok, kv_local, head_width)
    value_local = (value_near + landed[1]).reshape(group_tok, kv_local, head_width)
    attended_rows = attended_blk.reshape(group_tok, heads_local, head_width)
    query_rows = (
        (query_sum * score_scale).astype(jnp.bfloat16).reshape(group_tok, heads_local, head_width)
    )
    attended, query_grad = (
        lax.all_to_all(attended_rows, "uly", split_axis=0, concat_axis=1, tiled=True),
        lax.all_to_all(query_rows, "uly", split_axis=0, concat_axis=1, tiled=True),
    )
    key_parts, value_parts = (
        lax.all_to_all(key_local, "uly", split_axis=0, concat_axis=1, tiled=True),
        lax.all_to_all(value_local, "uly", split_axis=0, concat_axis=1, tiled=True),
    )
    key_gradient = jnp.sum(key_parts.reshape(tokens, kv_heads, copies, head_width), axis=2).astype(
        jnp.bfloat16
    )
    value_gradient = jnp.sum(
        value_parts.reshape(tokens, kv_heads, copies, head_width), axis=2
    ).astype(jnp.bfloat16)
    return (attended, query_grad, key_gradient, value_gradient)


def solution(mesh):
    placed = (
        P(("grp", "uly"), None, None),
        P(("grp", "uly"), None, None),
        P(("grp", "uly"), None, None),
        P(("grp", "uly"), None, None),
        P(),
        P(),
    )
    return jax.shard_map(
        on_device,
        mesh=mesh,
        in_specs=placed,
        out_specs=(
            P(("grp", "uly"), None, None),
            P(("grp", "uly"), None, None),
            P(("grp", "uly"), None, None),
            P(("grp", "uly"), None, None),
        ),
        check_vma=False,
    )
```

profile of v0, /device:TPU:0, one launch (start us, length us, event | category | flops | bytes accessed | tf_op | source)
XLA Modules:
  0.0 215.2 jit_solution(12773727700696270377)
XLA Ops:
  2.3 4.2 %all-to-all-start = ((bf16[128,4,128]{2,0,1:T(8,128)(2,1)}), bf16[128,4,128]{2,0,1:T(8,128)(2,1)S(1)}, u32[]{:S(2)}, u32[]{:S(2)}) async-start(bf16[128,4,128]{2,0,1:T(8,128)(2,1)} %copy.88), calls=%async_computation | async-start | bytes 262144 | tf_op jit(solution)/shard_map/all_to_all | solution.py:38
  15.4 3.4 %all-to-all-start.2 = ((bf16[128,4,128]{2,0,1:T(8,128)(2,1)}), bf16[128,4,128]{2,0,1:T(8,128)(2,1)S(1)}, u32[]{:S(2)}, u32[]{:S(2)}) async-start(bf16[128,4,128]{2,0,1:T(8,128)(2,1)} %copy.96), calls=%async_computation.2 | async-start | bytes 262144 | tf_op jit(solution)/shard_map/all_to_all | solution.py:39
  18.9 4.4 %all-to-all-done.2 = bf16[128,4,128]{2,0,1:T(8,128)(2,1)S(1)} async-done(((bf16[128,4,128]{2,0,1:T(8,128)(2,1)}), bf16[128,4,128]{2,0,1:T(8,128)(2,1)S(1)}, u32[]{:S(2)}, u32[]{:S(2)}) %all-to-all-start.2) | async-done | bytes 131104 | tf_op jit(solution)/shard_map/all_to_all | solution.py:39
  23.4 3.6 %all-to-all-start.1 = ((bf16[128,32,128]{2,0,1:T(8,128)(2,1)}), bf16[128,32,128]{2,0,1:T(8,128)(2,1)S(1)}, u32[]{:S(2)}, u32[]{:S(2)}) async-start(bf16[128,32,128]{2,0,1:T(8,128)(2,1)} %copy.90), calls=%async_computation.1 | async-start | bytes 2097152 | tf_op jit(solution)/shard_map/all_to_all | solution.py:36
  27.0 12.9 %all-to-all-done.1 = bf16[128,32,128]{2,0,1:T(8,128)(2,1)S(1)} async-done(((bf16[128,32,128]{2,0,1:T(8,128)(2,1)}), bf16[128,32,128]{2,0,1:T(8,128)(2,1)S(1)}, u32[]{:S(2)}, u32[]{:S(2)}) %all-to-all-start.1) | async-done | bytes 1048608 | tf_op jit(solution)/shard_map/all_to_all | solution.py:36
  39.9 3.6 %all-to-all-start.5 = ((bf16[128,32,128]{2,0,1:T(8,128)(2,1)}), bf16[128,32,128]{2,0,1:T(8,128)(2,1)S(1)}, u32[]{:S(2)}, u32[]{:S(2)}) async-start(bf16[128,32,128]{2,0,1:T(8,128)(2,1)} %copy.108), calls=%async_computation.5 | async-start | bytes 2097152 | tf_op jit(solution)/shard_map/all_to_all | solution.py:37
  45.9 9.7 %all-to-all-done.5 = bf16[128,32,128]{2,0,1:T(8,128)(2,1)S(1)} async-done(((bf16[128,32,128]{2,0,1:T(8,128)(2,1)}), bf16[128,32,128]{2,0,1:T(8,128)(2,1)S(1)}, u32[]{:S(2)}, u32[]{:S(2)}) %all-to-all-start.5) | async-done | bytes 1048608 | tf_op jit(solution)/shard_map/all_to_all | solution.py:37
  55.6 5.9 %all-to-all-start.3 = ((bf16[2,16,32,2,128]{4,2,3,0,1:T(8,128)(2,1)}), bf16[2,16,32,2,128]{4,2,3,0,1:T(8,128)(2,1)}, u32[]{:S(2)}, u32[]{:S(2)}) async-start(bf16[2,16,32,2,128]{4,2,3,0,1:T(8,128)(2,1)} %select_bitcast_fusion), calls=%async_computation.3 | async-start | bytes 1048576 | tf_op jit(solution)/shard_map/all_to_all | solution.py:43
  69.0 7.0 %all-to-all-done.3 = bf16[2,16,32,2,128]{4,2,3,0,1:T(8,128)(2,1)} async-done(((bf16[2,16,32,2,128]{4,2,3,0,1:T(8,128)(2,1)}), bf16[2,16,32,2,128]{4,2,3,0,1:T(8,128)(2,1)}, u32[]{:S(2)}, u32[]{:S(2)}) %all-to-all-start.3) | async-done | bytes 524320 | tf_op jit(solution)/shard_map/all_to_all | solution.py:43
  86.4 4.7 %while.43 = (s32[]{:T(128)}, f32[8,2,8,32]{3,2,1,0:T(8,128)S(1)}, f32[8,2,8,32]{3,2,1,0:T(8,128)}, s32[]{:T(128)}, pred[8,1]{0,1:T(4,128)(4,1)S(1)}, /*index=5*/f32[8,2,32,32,8]{3,4,2,1,0:T(8,128)}, s32[]{:T(128)}) while((s32[]{:T(128)}, f32[8,2,8,32]{3,2,1,0:T(8,128)S(1)}, f32[8,2,8,32]{3,2,1,0:T(8,128)}, s32[]{:T(128)}, ...), condition=%wide.region_7.9_spmd, body=%wide.region_4.8_spmd.sunk | while | flops 925698 | bytes 3489969 | solution.py:88
  92.0 3.5 %convolution_bitcast_fusion.1 = f32[8,32,2,8,128]{4,1,3,2,0:T(8,128)} fusion(f32[8,2,8,32,32]{3,4,2,1,0:T(8,128)} %copy-done.2, f32[8,2,8,32]{3,2,1,0:T(8,128)S(1)} %log_add_fusion, bf16[8,32,2,128,1]{3,1,0,2,4:T(8,128)(2,1)} %bitcast.260), kind=kOutput, calls=%fused_computation.52 | convolution fusion | flops 33816576 | bytes 2768896 | tf_op jit(solution)/shard_map/pkgqj,pjkd->pqkgd/dot_general | solution.py:94
  95.5 4.7 %while.44 = (s32[]{:T(128)}, f32[8,32,2,8,128]{4,1,3,2,0:T(8,128)}, s32[]{:T(128)}, pred[8,1]{0,1:T(4,128)(4,1)S(1)}, f32[8,2,32,32,8]{2,3,4,1,0:T(8,128)S(1)}, ...) while((s32[]{:T(128)}, f32[8,32,2,8,128]{4,1,3,2,0:T(8,128)}, s32[]{:T(128)}, ...), condition=%wide.region_9.11_spmd, body=%wide.region_8.10_spmd.sunk | while | flops 34603008 | bytes 4866141 | solution.py:108
  96.1 3.3 %bitcast_add_fusion.6 = f32[8,32,2,8,128]{4,1,3,2,0:T(8,128)} fusion(f32[8,32,2,8,128]{4,1,3,2,0:T(8,128)} %get-tuple-element.814, f32[8,2,32,32,8]{2,3,4,1,0:T(8,128)S(1)} %get-tuple-element.825, f32[8,2,8,32]{3,2,1,0:T(8,128)S(1)} %get-tuple-element.826, pred[8]{0:T(512)(128)(4,1)S(1)} %bitcast.277, bf16[8,32,2,128]{3,1,2,0:T(8,128)(2,1)S(1)} %get-tuple-element.827), kind=kOutput, calls=%fused_computation.9.clone.1 | convolution fusion | flops 34603008 | bytes 4866056 | tf_op jit(solution)/shard_map/while/body/pkgqj,pjkd->pqkgd/dot_general | solution.py:104
  107.6 3.3 %convolution_bitcast_fusion.4 = f32[1,8,32,2,128]{4,2,3,1,0:T(8,128)} fusion(f32[8,2,32,32,8]{3,2,4,1,0:T(8,128)} %copy-done.8, f32[8,2,8,32]{3,2,1,0:T(8,128)S(1)} %get-tuple-element.866, pred[8]{0:T(512)(128)(4,1)S(1)} %get-tuple-element.627, bf16[8,32,2,8,128]{4,3,2,1,0:T(8,128)(2,1)S(1)} %bitcast.245), kind=kOutput, calls=%fused_computation.56 | convolution fusion | flops 34078720 | bytes 1851400 | tf_op jit(solution)/shard_map/while/body/pkgqj,pqkgd->pjkd/dot_general | solution.py:129
  122.4 6.0 %while.45 = (s32[]{:T(128)}, f32[8,32,2,8,128]{4,1,3,2,0:T(8,128)}, f32[2,16,32,2,128]{4,3,2,1,0:T(2,128)S(1)}, s32[]{:T(128)}, pred[8,1]{0,1:T(4,128)(4,1)S(1)}...) while((s32[]{:T(128)}, f32[8,32,2,8,128]{4,1,3,2,0:T(8,128)}, ...), condition=%wide.region_12.14_spmd, body=%wide.region_11.13_spmd.sunk | while | flops 35127296 | bytes 12746905 | solution.py:154
  123.1 4.1 %bitcast_add_fusion.7 = f32[8,32,2,8,128]{4,1,3,2,0:T(8,128)} fusion(f32[8,32,2,8,128]{4,1,3,2,0:T(8,128)} %get-tuple-element.842, f32[8,2,32,32,8]{2,3,4,1,0:T(8,128)} %get-tuple-element.860, f32[8,2,32,32,8]{2,3,4,1,0:T(8,128)S(1)} %get-tuple-element.858, f32[8,2,8,32]{3,2,1,0:T(8,128)S(1)} %get-tuple-element.861, ...), kind=kOutput, calls=%fused_computation.20.clone.1 | convolution fusion | flops 34865152 | bytes 5406728 | tf_op jit(solution)/shard_map/while/body/pkgqj,pjkd->pqkgd/dot_general | solution.py:122
  128.4 4.0 %fusion.29 = bf16[8,32,2,8,128]{4,3,2,1,0:T(8,128)(2,1)} fusion(f32[8,32,2,8,128]{4,1,3,2,0:T(8,128)} %get-tuple-element.466), kind=kLoop, calls=%fused_computation.45 | loop fusion | flops 1048576 | bytes 3145728 | tf_op jit(solution)/shard_map/convert_element_type | solution.py:164
  132.4 3.6 %all-to-all-start.6 = ((bf16[256,16,128]{2,1,0:T(8,128)(2,1)}), bf16[256,16,128]{2,1,0:T(8,128)(2,1)S(1)}, u32[]{:S(2)}, u32[]{:S(2)}) async-start(bf16[256,16,128]{2,1,0:T(8,128)(2,1)} %bitcast.69), calls=%async_computation.6 | async-start | bytes 2097152 | tf_op jit(solution)/shard_map/all_to_all | solution.py:168
  136.1 13.9 %all-to-all-done.6 = bf16[256,16,128]{2,1,0:T(8,128)(2,1)S(1)} async-done(((bf16[256,16,128]{2,1,0:T(8,128)(2,1)}), bf16[256,16,128]{2,1,0:T(8,128)(2,1)S(1)}, u32[]{:S(2)}, u32[]{:S(2)}) %all-to-all-start.6) | async-done | bytes 1048608 | tf_op jit(solution)/shard_map/all_to_all | solution.py:168
  150.0 29.1 %all_to_all.124 = f32[2,16,32,2,128]{4,3,2,0,1:T(2,128)} all-to-all(f32[2,16,32,2,128]{4,3,2,0,1:T(2,128)S(1)} %copy.127), channel_id=1, replica_groups=mesh['grp'=16,'uly'=2] {'grp'}, dimensions={1} | all-to-all | bytes 2097152 | tf_op jit(solution)/shard_map/all_to_all | solution.py:158
  179.1 4.9 %all-to-all-start.4 = ((bf16[256,16,128]{2,1,0:T(8,128)(2,1)}), bf16[256,16,128]{2,1,0:T(8,128)(2,1)}, u32[]{:S(2)}, u32[]{:S(2)}) async-start(bf16[256,16,128]{2,1,0:T(8,128)(2,1)} %bitcast.252), calls=%async_computation.4 | async-start | bytes 2097152 | tf_op jit(solution)/shard_map/all_to_all | solution.py:167
  188.1 10.6 %all-to-all-done.4 = bf16[256,16,128]{2,1,0:T(8,128)(2,1)} async-done(((bf16[256,16,128]{2,1,0:T(8,128)(2,1)}), bf16[256,16,128]{2,1,0:T(8,128)(2,1)}, u32[]{:S(2)}, u32[]{:S(2)}) %all-to-all-start.4) | async-done | bytes 1048608 | tf_op jit(solution)/shard_map/all_to_all | solution.py:167
  198.7 3.4 %all-to-all-start.9 = ((bf16[256,2,128]{2,1,0:T(2,128)(2,1)}), bf16[256,2,128]{2,1,0:T(2,128)(2,1)S(1)}, u32[]{:S(2)}, u32[]{:S(2)}) async-start(bf16[256,2,128]{2,1,0:T(2,128)(2,1)} %copy.136), calls=%async_computation.9 | async-start | bytes 262144 | tf_op jit(solution)/shard_map/all_to_all | solution.py:172
  206.6 3.4 %all-to-all-start.8 = ((bf16[256,2,128]{2,1,0:T(2,128)(2,1)}), bf16[256,2,128]{2,1,0:T(2,128)(2,1)S(1)}, u32[]{:S(2)}, u32[]{:S(2)}) async-start(bf16[256,2,128]{2,1,0:T(2,128)(2,1)} %copy.131), calls=%async_computation.8 | async-start | bytes 262144 | tf_op jit(solution)/shard_map/all_to_all | solution.py:171
  (133 shorter events, 68.2 us)
Async XLA Ops:
  0.6 13.4 %copy-start.24 = (bf16[128,32,128]{2,1,0:T(8,128)(2,1)S(1)}, bf16[128,32,128]{2,1,0:T(8,128)(2,1)}, u32[]{:S(2)}) copy-start(bf16[128,32,128]{2,1,0:T(8,128)(2,1)} %param.17) | copy-start | bytes 3145732
  2.3 13.1 %all-to-all-start = ((bf16[128,4,128]{2,0,1:T(8,128)(2,1)}), bf16[128,4,128]{2,0,1:T(8,128)(2,1)S(1)}, u32[]{:S(2)}, u32[]{:S(2)}) async-start(bf16[128,4,128]{2,0,1:T(8,128)(2,1)} %copy.88), calls=%async_computation | async-start | bytes 262144 | tf_op jit(solution)/shard_map/all_to_all | solution.py:38
  15.4 7.9 %all-to-all-start.2 = ((bf16[128,4,128]{2,0,1:T(8,128)(2,1)}), bf16[128,4,128]{2,0,1:T(8,128)(2,1)S(1)}, u32[]{:S(2)}, u32[]{:S(2)}) async-start(bf16[128,4,128]{2,0,1:T(8,128)(2,1)} %copy.96), calls=%async_computation.2 | async-start | bytes 262144 | tf_op jit(solution)/shard_map/all_to_all | solution.py:39
  18.9 21.0 %copy-start.27 = (s32[16]{0:T(128)}, s32[16]{0:T(128)S(1)}, u32[]{:S(2)}) copy-start(s32[16]{0:T(128)S(1)} %fusion.72) | copy-start | bytes 196
  23.4 16.6 %all-to-all-start.1 = ((bf16[128,32,128]{2,0,1:T(8,128)(2,1)}), bf16[128,32,128]{2,0,1:T(8,128)(2,1)S(1)}, u32[]{:S(2)}, u32[]{:S(2)}) async-start(bf16[128,32,128]{2,0,1:T(8,128)(2,1)} %copy.90), calls=%async_computation.1 | async-start | bytes 2097152 | tf_op jit(solution)/shard_map/all_to_all | solution.py:36
  39.9 15.7 %all-to-all-start.5 = ((bf16[128,32,128]{2,0,1:T(8,128)(2,1)}), bf16[128,32,128]{2,0,1:T(8,128)(2,1)S(1)}, u32[]{:S(2)}, u32[]{:S(2)}) async-start(bf16[128,32,128]{2,0,1:T(8,128)(2,1)} %copy.108), calls=%async_computation.5 | async-start | bytes 2097152 | tf_op jit(solution)/shard_map/all_to_all | solution.py:37
  44.2 20.4 %copy-start.19 = (bf16[2,128,2,128]{3,1,0,2:T(8,128)(2,1)}, bf16[2,128,2,128]{3,1,0,2:T(8,128)(2,1)S(1)}, u32[]{:S(2)}) copy-start(bf16[2,128,2,128]{3,1,0,2:T(8,128)(2,1)S(1)} %copy.89) | copy-start | bytes 393220
  44.2 11.4 %copy-start.21 = (bf16[2,128,2,128]{3,1,0,2:T(8,128)(2,1)}, bf16[2,128,2,128]{3,1,0,2:T(8,128)(2,1)S(1)}, u32[]{:S(2)}) copy-start(bf16[2,128,2,128]{3,1,0,2:T(8,128)(2,1)S(1)} %copy.97) | copy-start | bytes 393220
  55.6 6.7 %copy-start.16 = (bf16[128,32,128]{2,0,1:T(8,128)(2,1)}, bf16[128,32,128]{2,0,1:T(8,128)(2,1)S(1)}, u32[]{:S(2)}) copy-start(bf16[128,32,128]{2,0,1:T(8,128)(2,1)S(1)} %all-to-all-done.5) | copy-start | bytes 3145732
  55.6 20.4 %all-to-all-start.3 = ((bf16[2,16,32,2,128]{4,2,3,0,1:T(8,128)(2,1)}), bf16[2,16,32,2,128]{4,2,3,0,1:T(8,128)(2,1)}, u32[]{:S(2)}, u32[]{:S(2)}) async-start(bf16[2,16,32,2,128]{4,2,3,0,1:T(8,128)(2,1)} %select_bitcast_fusion), calls=%async_computation.3 | async-start | bytes 1048576 | tf_op jit(solution)/shard_map/all_to_all | solution.py:43
  62.3 16.1 %copy-start.10 = (bf16[2,128,16,128]{3,2,1,0:T(8,128)(2,1)}, bf16[2,128,16,128]{3,2,1,0:T(8,128)(2,1)S(1)}, u32[]{:S(2)}) copy-start(bf16[2,128,16,128]{3,2,1,0:T(8,128)(2,1)S(1)} %copy.92) | copy-start | bytes 3145732
  64.6 46.3 %copy-start.6 = (bf16[2,128,16,128]{3,2,1,0:T(8,128)(2,1)}, bf16[2,128,16,128]{3,2,1,0:T(8,128)(2,1)S(1)}, u32[]{:S(2)}) copy-start(bf16[2,128,16,128]{3,2,1,0:T(8,128)(2,1)S(1)} %copy.110) | copy-start | bytes 3145732
  107.6 6.1 %copy-start.12 = (f32[8,2,32,32,8]{3,2,4,1,0:T(8,128)S(1)}, f32[8,2,32,32,8]{3,2,4,1,0:T(8,128)}, u32[]{:S(2)}) copy-start(f32[8,2,32,32,8]{3,2,4,1,0:T(8,128)} %fusion.52) | copy-start | bytes 1572868
  123.0 4.1 %copy-start.5 = (f32[2,32,2,128,16]{3,2,1,4,0:T(2,128)S(1)}, f32[2,32,2,128,16]{3,2,1,4,0:T(2,128)}, u32[]{:S(2)}) copy-start(f32[2,32,2,128,16]{3,2,1,4,0:T(2,128)} %get-tuple-element.863) | copy-start | bytes 3145732 | tf_op jit(solution)/shard_map/while
  132.4 17.6 %all-to-all-start.6 = ((bf16[256,16,128]{2,1,0:T(8,128)(2,1)}), bf16[256,16,128]{2,1,0:T(8,128)(2,1)S(1)}, u32[]{:S(2)}, u32[]{:S(2)}) async-start(bf16[256,16,128]{2,1,0:T(8,128)(2,1)} %bitcast.69), calls=%async_computation.6 | async-start | bytes 2097152 | tf_op jit(solution)/shard_map/all_to_all | solution.py:168
  136.1 48.0 %copy-start.26 = (pred[16]{0:T(512)(128)(4,1)S(1)}, pred[16]{0:T(512)(128)(4,1)}, u32[]{:S(2)}) copy-start(pred[16]{0:T(512)(128)(4,1)} %get-tuple-element.620) | copy-start | bytes 52
  136.1 48.0 %copy-start.28 = (s32[16]{0:T(128)S(1)}, s32[16]{0:T(128)}, u32[]{:S(2)}) copy-start(s32[16]{0:T(128)} %copy-done.27) | copy-start | bytes 196
  150.0 29.1 %copy-start.14 = (bf16[256,16,128]{2,1,0:T(8,128)(2,1)}, bf16[256,16,128]{2,1,0:T(8,128)(2,1)S(1)}, u32[]{:S(2)}) copy-start(bf16[256,16,128]{2,1,0:T(8,128)(2,1)S(1)} %all-to-all-done.6) | copy-start | bytes 3145732
  179.1 7.4 %copy-start.4 = (f32[8,2,8,32,32]{3,4,2,1,0:T(8,128)S(1)}, f32[8,2,8,32,32]{3,4,2,1,0:T(8,128)}, u32[]{:S(2)}) copy-start(f32[8,2,8,32,32]{3,4,2,1,0:T(8,128)} %copy-done.2) | copy-start | bytes 1572868
  179.1 7.4 %copy-start.7 = (bf16[2,128,16,128]{3,2,1,0:T(8,128)(2,1)S(1)}, bf16[2,128,16,128]{3,2,1,0:T(8,128)(2,1)}, u32[]{:S(2)}) copy-start(bf16[2,128,16,128]{3,2,1,0:T(8,128)(2,1)} %copy-done.6) | copy-start | bytes 3145732
  179.1 19.6 %all-to-all-start.4 = ((bf16[256,16,128]{2,1,0:T(8,128)(2,1)}), bf16[256,16,128]{2,1,0:T(8,128)(2,1)}, u32[]{:S(2)}, u32[]{:S(2)}) async-start(bf16[256,16,128]{2,1,0:T(8,128)(2,1)} %bitcast.252), calls=%async_computation.4 | async-start | bytes 2097152 | tf_op jit(solution)/shard_map/all_to_all | solution.py:167
  187.3 22.6 %copy-start.15 = (bf16[256,16,128]{2,1,0:T(8,128)(2,1)S(1)}, bf16[256,16,128]{2,1,0:T(8,128)(2,1)}, u32[]{:S(2)}) copy-start(bf16[256,16,128]{2,1,0:T(8,128)(2,1)} %copy-done.14) | copy-start | bytes 3145732
  198.7 7.8 %all-to-all-start.9 = ((bf16[256,2,128]{2,1,0:T(2,128)(2,1)}), bf16[256,2,128]{2,1,0:T(2,128)(2,1)S(1)}, u32[]{:S(2)}, u32[]{:S(2)}) async-start(bf16[256,2,128]{2,1,0:T(2,128)(2,1)} %copy.136), calls=%async_computation.9 | async-start | bytes 262144 | tf_op jit(solution)/shard_map/all_to_all | solution.py:172
  206.6 7.8 %all-to-all-start.8 = ((bf16[256,2,128]{2,1,0:T(2,128)(2,1)}), bf16[256,2,128]{2,1,0:T(2,128)(2,1)S(1)}, u32[]{:S(2)}, u32[]{:S(2)}) async-start(bf16[256,2,128]{2,1,0:T(2,128)(2,1)} %copy.131), calls=%async_computation.8 | async-start | bytes 262144 | tf_op jit(solution)/shard_map/all_to_all | solution.py:171
  (14 other events, 32.2 us)
where the time goes:
time: 217 us; the launch traced here: 215 us
  waiting for transfers between devices  60.3 us (28%)
  starting transfers between devices  35.9 us (17%)
  local copies, waits for them, and re-layouts  35.3 us (16%)
  matrix products  32.2 us (15%)
  blocking collectives  29.1 us (13%)
  other arithmetic  17.1 us (8%)
  loops' own time  4.02 us (2%)
    all_to_all x1, blocking collectives, on_device(): lax.all_to_all(far_grads, 'grp', split_axis=1, concat_axis=1, tiled=True)  29.1 us
    all_to_all x1, waiting for transfers between devices, on_device(): lax.all_to_all(query_rows, 'uly', split_axis=0, concat_axis=1, tiled=True)  13.9 us
    all_to_all x1, waiting for transfers between devices, on_device(): lax.all_to_all(queries, 'uly', split_axis=1, concat_axis=0, tiled=True)  12.9 us
    unnamed x57, local copies, waits for them, and re-layouts  12.2 us
    all_to_all x1, waiting for transfers between devices, on_device(): lax.all_to_all(attended_rows, 'uly', split_axis=0, concat_axis=1, tiled=T...  10.6 us
    all_to_all x1, waiting for transfers between devices, on_device(): lax.all_to_all(output_cotangent, 'uly', split_axis=1, concat_axis=0, tile...  9.72 us
    all_to_all x1, waiting for transfers between devices, on_device(): lax.all_to_all(outgoing, 'grp', split_axis=1, concat_axis=1, tiled=True)  7.02 us
    dot_general x2, matrix products, backward(): jnp.einsum('pkgqj,pjkd->pqkgd', dscores, key_rows, preferred_element_type...  5.96 us
  transfers between devices with their start and end apart: 9, of which 8 were waited for; matrix products, arithmetic and copies ran while one was open for 13% of the time, Pallas kernels for 0%

commit v1 on v0

--- a/solution.py
+++ b/solution.py
@@ -2,6 +2,28 @@
 import jax.numpy as jnp
 from jax import lax
 from jax.sharding import PartitionSpec as P
+
+
+def cut_along(x, dim, count):
+    before, after = (x.shape[:dim], x.shape[dim + 1 :])
+    return jnp.moveaxis(x.reshape(*before, count, -1, *after), dim, 0)
+
+
+def laid_out(parts, dim):
+    dims = list(parts.shape[1:])
+    dims[dim] *= parts.shape[0]
+    return jnp.moveaxis(parts, 0, dim).reshape(dims)
+
+
+def exchange_in_pairs(x, axis, split_dim, concat_dim):
+    length, place = (lax.axis_size(axis), lax.axis_index(axis))
+    parts = cut_along(x, split_dim, length)
+    finished = [parts[place]]
+    for step in range(1, length):
+        sent = parts[place ^ step]
+        finished.append(lax.ppermute(sent, axis, [(i, i ^ step) for i in range(length)]))
+    parts = jnp.stack(finished)[place ^ jnp.arange(length)]
+    return laid_out(parts, concat_dim)
 
 
 def on_device(queries, keys, values, output_cotangent, block_lists, list_counts):
@@ -40,7 +62,7 @@
     )
     stacked = jnp.stack([to_blocks(key_heads), to_blocks(value_heads)])
     outgoing = jnp.take(stacked, send_place, axis=1)
-    arrived = lax.all_to_all(outgoing, "grp", split_axis=1, concat_axis=1, tiled=True)
+    arrived = exchange_in_pairs(outgoing, "grp", 1, 1)
     kv_local = key_heads.shape[1]
     heads_local = query_heads.shape[1]
     heads_per_group = heads_local // kv_local

time: 217 us -> 208 us (0.959)
  waiting for transfers between devices: 60.3 us -> 37.4 us
  starting transfers between devices: 35.9 us -> 52.3 us
  other arithmetic: 17.1 us -> 14.4 us
    ppermute x0 -> x15, starting transfers between devices: none -> 21.7 us  [exchange_in_pairs(): lax.ppermute(sent, axis, [(i, i ^ step) for i in range(length)])]
    all_to_all x1, waiting for transfers between devices: 12.9 us -> 0.01 us  [on_device(): lax.all_to_all(queries, 'uly', split_axis=1, concat_axis=0, tiled=True)]
    all_to_all x1, waiting for transfers between devices: 9.72 us -> 0.01 us  [on_device(): lax.all_to_all(output_cotangent, 'uly', split_axis=1, concat_axis=0, tile...]
    all_to_all x1 -> x0, waiting for transfers between devices: 7.02 us -> none  [on_device(): lax.all_to_all(outgoing, 'grp', split_axis=1, concat_axis=1, tiled=True)]
    ppermute x0 -> x15, waiting for transfers between devices: none -> 5.92 us  [exchange_in_pairs(): lax.ppermute(sent, axis, [(i, i ^ step) for i in range(length)])]
    all_to_all x1 -> x0, starting transfers between devices: 5.91 us -> none  [on_device(): lax.all_to_all(outgoing, 'grp', split_axis=1, concat_axis=1, tiled=True)]
    unnamed x57 -> x66, local copies, waits for them, and re-layouts: 12.2 us -> 12.9 us
  transfers between devices with their start and end apart: 9 -> 23, of which waited for: 8 -> 8; matrix products, arithmetic and copies ran while one was open for 13% -> 21% of each run, Pallas kernels for 0% -> 0%
where the time goes in v1:
time: 208 us; the launch traced here: 206 us
  starting transfers between devices  52.3 us (25%)
  waiting for transfers between devices  37.4 us (18%)
  local copies, waits for them, and re-layouts  34.9 us (17%)
  matrix products  33.2 us (16%)
  blocking collectives  28.3 us (14%)
  other arithmetic  14.4 us (7%)
  loops' own time  4.34 us (2%)
    all_to_all x1, blocking collectives, on_device(): lax.all_to_all(far_grads, 'grp', split_axis=1, concat_axis=1, tiled=True)  28.3 us
    ppermute x15, starting transfers between devices, exchange_in_pairs(): lax.ppermute(sent, axis, [(i, i ^ step) for i in range(length)])  21.7 us
    all_to_all x1, waiting for transfers between devices, on_device(): lax.all_to_all(query_rows, 'uly', split_axis=0, concat_axis=1, tiled=True)  14.4 us
    unnamed x66, local copies, waits for them, and re-layouts  12.9 us
    all_to_all x1, waiting for transfers between devices, on_device(): lax.all_to_all(attended_rows, 'uly', split_axis=0, concat_axis=1, tiled=T...  10.9 us
    dot_general x2, matrix products, backward(): jnp.einsum('pkgqj,pjkd->pqkgd', dscores, key_rows, preferred_element_type...  6.01 us
    dot_general x2, matrix products, backward(): jnp.einsum('pqkgd,pjkd->pkgqj', grad_blk, value_rows, preferred_element_t...  5.95 us
    ppermute x15, waiting for transfers between devices, exchange_in_pairs(): lax.ppermute(sent, axis, [(i, i ^ step) for i in range(length)])  5.92 us
  transfers between devices with their start and end apart: 23, of which 8 were waited for; matrix products, arithmetic and copies ran while one was open for 21% of the time, Pallas kernels for 0%

profile of v1, /device:TPU:0, one launch (start us, length us, event | category | flops | bytes accessed | tf_op | source)
XLA Modules:
  0.0 206.2 jit_solution(7025686496187461987)
XLA Ops:
  2.3 4.2 %all-to-all-start = ((bf16[128,4,128]{2,0,1:T(8,128)(2,1)}), bf16[128,4,128]{2,0,1:T(8,128)(2,1)S(1)}, u32[]{:S(2)}, u32[]{:S(2)}) async-start(bf16[128,4,128]{2,0,1:T(8,128)(2,1)} %copy.90), calls=%async_computation | async-start | bytes 262144 | tf_op jit(solution)/shard_map/all_to_all | solution.py:60
  15.9 3.4 %all-to-all-start.2 = ((bf16[128,4,128]{2,0,1:T(8,128)(2,1)}), bf16[128,4,128]{2,0,1:T(8,128)(2,1)S(1)}, u32[]{:S(2)}, u32[]{:S(2)}) async-start(bf16[128,4,128]{2,0,1:T(8,128)(2,1)} %copy.98), calls=%async_computation.2 | async-start | bytes 262144 | tf_op jit(solution)/shard_map/all_to_all | solution.py:61
  19.3 4.5 %all-to-all-done.2 = bf16[128,4,128]{2,0,1:T(8,128)(2,1)S(1)} async-done(((bf16[128,4,128]{2,0,1:T(8,128)(2,1)}), bf16[128,4,128]{2,0,1:T(8,128)(2,1)S(1)}, u32[]{:S(2)}, u32[]{:S(2)}) %all-to-all-start.2) | async-done | bytes 131104 | tf_op jit(solution)/shard_map/all_to_all | solution.py:61
  23.8 3.6 %all-to-all-start.1 = ((bf16[128,32,128]{2,0,1:T(8,128)(2,1)}), bf16[128,32,128]{2,0,1:T(8,128)(2,1)S(1)}, u32[]{:S(2)}, u32[]{:S(2)}) async-start(bf16[128,32,128]{2,0,1:T(8,128)(2,1)} %copy.92), calls=%async_computation.1 | async-start | bytes 2097152 | tf_op jit(solution)/shard_map/all_to_all | solution.py:58
  39.0 3.3 %collective-permute-start.9 = (bf16[2,1,32,2,128]{4,2,3,0,1:T(8,128)(2,1)S(1)}, bf16[2,1,32,2,128]{4,2,3,0,1:T(8,128)(2,1)S(1)}, u32[]{:S(2)}, u32[]{:S(2)}) collective-permute-start(bf16[2,1,32,2,128]{4,2,3,0,1:T(8,128)(2,1)S(1)} %get-tuple-element.635), channel_id=1, source_target_pairs={{0,20},{2,22},{4,16},{6,18},{8,28},{10,30},{12,24},{14,26},{16,4},... | collective-permute-start | bytes 98312 | tf_op jit(solution)/shard_map/ppermute | solution.py:24
  42.5 3.7 %collective-permute-start.11 = (bf16[2,1,32,2,128]{4,2,3,0,1:T(8,128)(2,1)S(1)}, bf16[2,1,32,2,128]{4,2,3,0,1:T(8,128)(2,1)S(1)}, u32[]{:S(2)}, u32[]{:S(2)}) collective-permute-start(bf16[2,1,32,2,128]{4,2,3,0,1:T(8,128)(2,1)S(1)} %get-tuple-element.633), channel_id=1, source_target_pairs={{0,24},{2,26},{4,28},{6,30},{8,16},{10,18},{12,20},{14,22},{16,8},... | collective-permute-start | bytes 98312 | tf_op jit(solution)/shard_map/ppermute | solution.py:24
  46.4 4.3 %collective-permute-start.13 = (bf16[2,1,32,2,128]{4,2,3,0,1:T(8,128)(2,1)S(1)}, bf16[2,1,32,2,128]{4,2,3,0,1:T(8,128)(2,1)S(1)}, u32[]{:S(2)}, u32[]{:S(2)}) collective-permute-start(bf16[2,1,32,2,128]{4,2,3,0,1:T(8,128)(2,1)S(1)} %get-tuple-element.631), channel_id=1, source_target_pairs={{0,28},{2,30},{4,24},{6,26},{8,20},{10,22},{12,16},{14,18},{16,12}... | collective-permute-start | bytes 98312 | tf_op jit(solution)/shard_map/ppermute | solution.py:24
  53.5 3.4 %collective-permute-done.14 = bf16[2,1,32,2,128]{4,2,3,0,1:T(8,128)(2,1)S(1)} collective-permute-done((bf16[2,1,32,2,128]{4,2,3,0,1:T(8,128)(2,1)S(1)}, bf16[2,1,32,2,128]{4,2,3,0,1:T(8,128)(2,1)S(1)}, u32[]{:S(2)}, u32[]{:S(2)}) %collective-permute-start.14) | collective-permute-done | bytes 32800 | tf_op jit(solution)/shard_map/ppermute | solution.py:24
  58.9 4.4 %all-to-all-start.4 = ((bf16[128,32,128]{2,0,1:T(8,128)(2,1)}), bf16[128,32,128]{2,0,1:T(8,128)(2,1)}, u32[]{:S(2)}, u32[]{:S(2)}) async-start(bf16[128,32,128]{2,0,1:T(8,128)(2,1)} %copy.110), calls=%async_computation.4 | async-start | bytes 2097152 | tf_op jit(solution)/shard_map/all_to_all | solution.py:59
  76.8 4.2 %while.43 = (s32[]{:T(128)}, f32[8,2,8,32]{3,2,1,0:T(8,128)S(1)}, f32[8,2,8,32]{3,2,1,0:T(8,128)S(1)}, s32[]{:T(128)}, pred[8,1]{0,1:T(4,128)(4,1)S(1)}, /*index=5*/f32[8,2,32,32,8]{3,4,2,1,0:T(8,128)}, s32[]{:T(128)}) while((s32[]{:T(128)}, f32[8,2,8,32]{3,2,1,0:T(8,128)S(1)}, f32[8,2,8,32]{3,2,1,0:T(8,128)S(1)}, s32[]{:T(128)}, ...), condition=%wide.region_7.9_spmd, body=%wide.region_4.8_spmd.sunk | while | flops 925698 | bytes 3358841 | solution.py:110
  81.1 3.5 %convolution_bitcast_fusion.1 = f32[8,32,2,8,128]{4,1,3,2,0:T(8,128)} fusion(f32[8,2,8,32,32]{3,4,2,1,0:T(8,128)} %copy-done.2, f32[8,2,8,32]{3,2,1,0:T(8,128)S(1)} %log_add_fusion, bf16[8,32,2,128,1]{3,1,0,2,4:T(8,128)(2,1)S(1)} %bitcast.325), kind=kOutput, calls=%fused_computation.53 | convolution fusion | flops 33816576 | bytes 2768896 | tf_op jit(solution)/shard_map/pkgqj,pjkd->pqkgd/dot_general | solution.py:116
  84.6 4.8 %while.44 = (s32[]{:T(128)}, f32[8,32,2,8,128]{4,1,3,2,0:T(8,128)}, s32[]{:T(128)}, pred[8,1]{0,1:T(4,128)(4,1)S(1)}, f32[8,2,32,32,8]{2,3,4,1,0:T(8,128)S(1)}, ...) while((s32[]{:T(128)}, f32[8,32,2,8,128]{4,1,3,2,0:T(8,128)}, s32[]{:T(128)}, ...), condition=%wide.region_9.11_spmd, body=%wide.region_8.10_spmd.sunk | while | flops 34603008 | bytes 4866141 | solution.py:130
  85.3 3.3 %bitcast_add_fusion.6 = f32[8,32,2,8,128]{4,1,3,2,0:T(8,128)} fusion(f32[8,32,2,8,128]{4,1,3,2,0:T(8,128)} %get-tuple-element.831, f32[8,2,32,32,8]{2,3,4,1,0:T(8,128)S(1)} %get-tuple-element.842, f32[8,2,8,32]{3,2,1,0:T(8,128)S(1)} %get-tuple-element.843, pred[8]{0:T(512)(128)(4,1)S(1)} %bitcast.344, bf16[8,32,2,128]{3,1,2,0:T(8,128)(2,1)S(1)} %get-tuple-element.844), kind=kOutput, calls=%fused_computation.10.clone.1 | convolution fusion | flops 34603008 | bytes 4866056 | tf_op jit(solution)/shard_map/while/body/pkgqj,pjkd->pqkgd/dot_general | solution.py:126
  98.8 3.3 %convolution_bitcast_fusion.4 = f32[1,8,32,2,128]{4,2,3,1,0:T(8,128)} fusion(f32[8,2,32,32,8]{3,2,4,1,0:T(8,128)} %copy-done.8, f32[8,2,8,32]{3,2,1,0:T(8,128)S(1)} %get-tuple-element.883, pred[8]{0:T(512)(128)(4,1)S(1)} %get-tuple-element.627, bf16[8,32,2,8,128]{4,3,2,1,0:T(8,128)(2,1)S(1)} %bitcast.311), kind=kOutput, calls=%fused_computation.57 | convolution fusion | flops 34078720 | bytes 1851400 | tf_op jit(solution)/shard_map/while/body/pkgqj,pqkgd->pjkd/dot_general | solution.py:151
  113.7 6.1 %while.45 = (s32[]{:T(128)}, f32[8,32,2,8,128]{4,1,3,2,0:T(8,128)}, f32[2,16,32,2,128]{4,3,2,1,0:T(2,128)S(1)}, s32[]{:T(128)}, pred[8,1]{0,1:T(4,128)(4,1)S(1)}...) while((s32[]{:T(128)}, f32[8,32,2,8,128]{4,1,3,2,0:T(8,128)}, ...), condition=%wide.region_12.14_spmd, body=%wide.region_11.13_spmd.sunk | while | flops 35127296 | bytes 12746905 | solution.py:176
  114.4 4.1 %bitcast_add_fusion.7 = f32[8,32,2,8,128]{4,1,3,2,0:T(8,128)} fusion(f32[8,32,2,8,128]{4,1,3,2,0:T(8,128)} %get-tuple-element.859, f32[8,2,32,32,8]{2,3,4,1,0:T(8,128)} %get-tuple-element.877, f32[8,2,32,32,8]{2,3,4,1,0:T(8,128)S(1)} %get-tuple-element.875, f32[8,2,8,32]{3,2,1,0:T(8,128)S(1)} %get-tuple-element.878, ...), kind=kOutput, calls=%fused_computation.21.clone.1 | convolution fusion | flops 34865152 | bytes 5406728 | tf_op jit(solution)/shard_map/while/body/pkgqj,pjkd->pqkgd/dot_general | solution.py:144
  119.8 3.9 %fusion.29 = bf16[8,32,2,8,128]{4,3,2,1,0:T(8,128)(2,1)} fusion(f32[8,32,2,8,128]{4,1,3,2,0:T(8,128)} %get-tuple-element.466), kind=kLoop, calls=%fused_computation.46 | loop fusion | flops 1048576 | bytes 3145728 | tf_op jit(solution)/shard_map/convert_element_type | solution.py:186
  123.8 3.6 %all-to-all-start.5 = ((bf16[256,16,128]{2,1,0:T(8,128)(2,1)}), bf16[256,16,128]{2,1,0:T(8,128)(2,1)S(1)}, u32[]{:S(2)}, u32[]{:S(2)}) async-start(bf16[256,16,128]{2,1,0:T(8,128)(2,1)} %bitcast.106), calls=%async_computation.5 | async-start | bytes 2097152 | tf_op jit(solution)/shard_map/all_to_all | solution.py:190
  127.5 14.4 %all-to-all-done.5 = bf16[256,16,128]{2,1,0:T(8,128)(2,1)S(1)} async-done(((bf16[256,16,128]{2,1,0:T(8,128)(2,1)}), bf16[256,16,128]{2,1,0:T(8,128)(2,1)S(1)}, u32[]{:S(2)}, u32[]{:S(2)}) %all-to-all-start.5) | async-done | bytes 1048608 | tf_op jit(solution)/shard_map/all_to_all | solution.py:190
  141.8 28.3 %all_to_all.119 = f32[2,16,32,2,128]{4,3,2,0,1:T(2,128)} all-to-all(f32[2,16,32,2,128]{4,3,2,0,1:T(2,128)S(1)} %copy.129), channel_id=1, replica_groups=mesh['grp'=16,'uly'=2] {'grp'}, dimensions={1} | all-to-all | bytes 2097152 | tf_op jit(solution)/shard_map/all_to_all | solution.py:180
  170.1 4.7 %all-to-all-start.3 = ((bf16[256,16,128]{2,1,0:T(8,128)(2,1)}), bf16[256,16,128]{2,1,0:T(8,128)(2,1)}, u32[]{:S(2)}, u32[]{:S(2)}) async-start(bf16[256,16,128]{2,1,0:T(8,128)(2,1)} %bitcast.318), calls=%async_computation.3 | async-start | bytes 2097152 | tf_op jit(solution)/shard_map/all_to_all | solution.py:189
  178.9 10.9 %all-to-all-done.3 = bf16[256,16,128]{2,1,0:T(8,128)(2,1)} async-done(((bf16[256,16,128]{2,1,0:T(8,128)(2,1)}), bf16[256,16,128]{2,1,0:T(8,128)(2,1)}, u32[]{:S(2)}, u32[]{:S(2)}) %all-to-all-start.3) | async-done | bytes 1048608 | tf_op jit(solution)/shard_map/all_to_all | solution.py:189
  189.7 3.4 %all-to-all-start.8 = ((bf16[256,2,128]{2,1,0:T(2,128)(2,1)}), bf16[256,2,128]{2,1,0:T(2,128)(2,1)S(1)}, u32[]{:S(2)}, u32[]{:S(2)}) async-start(bf16[256,2,128]{2,1,0:T(2,128)(2,1)} %copy.138), calls=%async_computation.8 | async-start | bytes 262144 | tf_op jit(solution)/shard_map/all_to_all | solution.py:194
  197.6 3.4 %all-to-all-start.7 = ((bf16[256,2,128]{2,1,0:T(2,128)(2,1)}), bf16[256,2,128]{2,1,0:T(2,128)(2,1)S(1)}, u32[]{:S(2)}, u32[]{:S(2)}) async-start(bf16[256,2,128]{2,1,0:T(2,128)(2,1)} %copy.133), calls=%async_computation.7 | async-start | bytes 262144 | tf_op jit(solution)/shard_map/all_to_all | solution.py:193
  (170 shorter events, 79.0 us)
Async XLA Ops:
  2.3 13.6 %all-to-all-start = ((bf16[128,4,128]{2,0,1:T(8,128)(2,1)}), bf16[128,4,128]{2,0,1:T(8,128)(2,1)S(1)}, u32[]{:S(2)}, u32[]{:S(2)}) async-start(bf16[128,4,128]{2,0,1:T(8,128)(2,1)} %copy.90), calls=%async_computation | async-start | bytes 262144 | tf_op jit(solution)/shard_map/all_to_all | solution.py:60
  15.9 7.9 %all-to-all-start.2 = ((bf16[128,4,128]{2,0,1:T(8,128)(2,1)}), bf16[128,4,128]{2,0,1:T(8,128)(2,1)S(1)}, u32[]{:S(2)}, u32[]{:S(2)}) async-start(bf16[128,4,128]{2,0,1:T(8,128)(2,1)} %copy.98), calls=%async_computation.2 | async-start | bytes 262144 | tf_op jit(solution)/shard_map/all_to_all | solution.py:61
  23.8 35.0 %all-to-all-start.1 = ((bf16[128,32,128]{2,0,1:T(8,128)(2,1)}), bf16[128,32,128]{2,0,1:T(8,128)(2,1)S(1)}, u32[]{:S(2)}, u32[]{:S(2)}) async-start(bf16[128,32,128]{2,0,1:T(8,128)(2,1)} %copy.92), calls=%async_computation.1 | async-start | bytes 2097152 | tf_op jit(solution)/shard_map/all_to_all | solution.py:58
  29.1 4.1 %collective-permute-start = (bf16[2,1,32,2,128]{4,2,3,0,1:T(8,128)(2,1)S(1)}, bf16[2,1,32,2,128]{4,2,3,0,1:T(8,128)(2,1)S(1)}, u32[]{:S(2)}, u32[]{:S(2)}) collective-permute-start(bf16[2,1,32,2,128]{4,2,3,0,1:T(8,128)(2,1)S(1)} %get-tuple-element.644), channel_id=1, source_target_pairs={{0,2},{2,0},{4,6},{6,4},{8,10},{10,8},{12,14},{14,12},{16,18},{18,... | collective-permute-start | bytes 98312 | tf_op jit(solution)/shard_map/ppermute | solution.py:24
  29.2 6.6 %collective-permute-start.1 = (bf16[2,1,32,2,128]{4,2,3,0,1:T(8,128)(2,1)S(1)}, bf16[2,1,32,2,128]{4,2,3,0,1:T(8,128)(2,1)S(1)}, u32[]{:S(2)}, u32[]{:S(2)}) collective-permute-start(bf16[2,1,32,2,128]{4,2,3,0,1:T(8,128)(2,1)S(1)} %get-tuple-element.643), channel_id=1, source_target_pairs={{0,4},{2,6},{4,0},{6,2},{8,12},{10,14},{12,8},{14,10},{16,20},{18,... | collective-permute-start | bytes 98312 | tf_op jit(solution)/shard_map/ppermute | solution.py:24
  31.3 4.7 %collective-permute-start.2 = (bf16[2,1,32,2,128]{4,2,3,0,1:T(8,128)(2,1)S(1)}, bf16[2,1,32,2,128]{4,2,3,0,1:T(8,128)(2,1)S(1)}, u32[]{:S(2)}, u32[]{:S(2)}) collective-permute-start(bf16[2,1,32,2,128]{4,2,3,0,1:T(8,128)(2,1)S(1)} %get-tuple-element.642), channel_id=1, source_target_pairs={{0,6},{2,4},{4,2},{6,0},{8,14},{10,12},{12,10},{14,8},{16,22},{18,... | collective-permute-start | bytes 98312 | tf_op jit(solution)/shard_map/ppermute | solution.py:24
  31.3 7.4 %collective-permute-start.3 = (bf16[2,1,32,2,128]{4,2,3,0,1:T(8,128)(2,1)S(1)}, bf16[2,1,32,2,128]{4,2,3,0,1:T(8,128)(2,1)S(1)}, u32[]{:S(2)}, u32[]{:S(2)}) collective-permute-start(bf16[2,1,32,2,128]{4,2,3,0,1:T(8,128)(2,1)S(1)} %get-tuple-element.641), channel_id=1, source_target_pairs={{0,8},{2,10},{4,12},{6,14},{8,0},{10,2},{12,4},{14,6},{16,24},{18,... | collective-permute-start | bytes 98312 | tf_op jit(solution)/shard_map/ppermute | solution.py:24
  33.1 5.9 %collective-permute-start.4 = (bf16[2,1,32,2,128]{4,2,3,0,1:T(8,128)(2,1)S(1)}, bf16[2,1,32,2,128]{4,2,3,0,1:T(8,128)(2,1)S(1)}, u32[]{:S(2)}, u32[]{:S(2)}) collective-permute-start(bf16[2,1,32,2,128]{4,2,3,0,1:T(8,128)(2,1)S(1)} %get-tuple-element.640), channel_id=1, source_target_pairs={{0,10},{2,8},{4,14},{6,12},{8,2},{10,0},{12,6},{14,4},{16,26},{18,... | collective-permute-start | bytes 98312 | tf_op jit(solution)/shard_map/ppermute | solution.py:24
  33.1 9.2 %collective-permute-start.5 = (bf16[2,1,32,2,128]{4,2,3,0,1:T(8,128)(2,1)S(1)}, bf16[2,1,32,2,128]{4,2,3,0,1:T(8,128)(2,1)S(1)}, u32[]{:S(2)}, u32[]{:S(2)}) collective-permute-start(bf16[2,1,32,2,128]{4,2,3,0,1:T(8,128)(2,1)S(1)} %get-tuple-element.639), channel_id=1, source_target_pairs={{0,12},{2,14},{4,8},{6,10},{8,4},{10,6},{12,0},{14,2},{16,28},{18,... | collective-permute-start | bytes 98312 | tf_op jit(solution)/shard_map/ppermute | solution.py:24
  35.8 6.8 %collective-permute-start.6 = (bf16[2,1,32,2,128]{4,2,3,0,1:T(8,128)(2,1)S(1)}, bf16[2,1,32,2,128]{4,2,3,0,1:T(8,128)(2,1)S(1)}, u32[]{:S(2)}, u32[]{:S(2)}) collective-permute-start(bf16[2,1,32,2,128]{4,2,3,0,1:T(8,128)(2,1)S(1)} %get-tuple-element.638), channel_id=1, source_target_pairs={{0,14},{2,12},{4,10},{6,8},{8,6},{10,4},{12,2},{14,0},{16,30},{18,... | collective-permute-start | bytes 98312 | tf_op jit(solution)/shard_map/ppermute | solution.py:24
  35.9 10.3 %collective-permute-start.7 = (bf16[2,1,32,2,128]{4,2,3,0,1:T(8,128)(2,1)S(1)}, bf16[2,1,32,2,128]{4,2,3,0,1:T(8,128)(2,1)S(1)}, u32[]{:S(2)}, u32[]{:S(2)}) collective-permute-start(bf16[2,1,32,2,128]{4,2,3,0,1:T(8,128)(2,1)S(1)} %get-tuple-element.637), channel_id=1, source_target_pairs={{0,16},{2,18},{4,20},{6,22},{8,24},{10,26},{12,28},{14,30},{16,0},... | collective-permute-start | bytes 98312 | tf_op jit(solution)/shard_map/ppermute | solution.py:24
  38.7 7.7 %collective-permute-start.8 = (bf16[2,1,32,2,128]{4,2,3,0,1:T(8,128)(2,1)S(1)}, bf16[2,1,32,2,128]{4,2,3,0,1:T(8,128)(2,1)S(1)}, u32[]{:S(2)}, u32[]{:S(2)}) collective-permute-start(bf16[2,1,32,2,128]{4,2,3,0,1:T(8,128)(2,1)S(1)} %get-tuple-element.636), channel_id=1, source_target_pairs={{0,18},{2,16},{4,22},{6,20},{8,26},{10,24},{12,30},{14,28},{16,2},... | collective-permute-start | bytes 98312 | tf_op jit(solution)/shard_map/ppermute | solution.py:24
  39.0 11.8 %collective-permute-start.9 = (bf16[2,1,32,2,128]{4,2,3,0,1:T(8,128)(2,1)S(1)}, bf16[2,1,32,2,128]{4,2,3,0,1:T(8,128)(2,1)S(1)}, u32[]{:S(2)}, u32[]{:S(2)}) collective-permute-start(bf16[2,1,32,2,128]{4,2,3,0,1:T(8,128)(2,1)S(1)} %get-tuple-element.635), channel_id=1, source_target_pairs={{0,20},{2,22},{4,16},{6,18},{8,28},{10,30},{12,24},{14,26},{16,4},... | collective-permute-start | bytes 98312 | tf_op jit(solution)/shard_map/ppermute | solution.py:24
  42.4 8.6 %collective-permute-start.10 = (bf16[2,1,32,2,128]{4,2,3,0,1:T(8,128)(2,1)S(1)}, bf16[2,1,32,2,128]{4,2,3,0,1:T(8,128)(2,1)S(1)}, u32[]{:S(2)}, u32[]{:S(2)}) collective-permute-start(bf16[2,1,32,2,128]{4,2,3,0,1:T(8,128)(2,1)S(1)} %get-tuple-element.634), channel_id=1, source_target_pairs={{0,22},{2,20},{4,18},{6,16},{8,30},{10,28},{12,26},{14,24},{16,6},... | collective-permute-start | bytes 98312 | tf_op jit(solution)/shard_map/ppermute | solution.py:24
  42.5 8.4 %collective-permute-start.11 = (bf16[2,1,32,2,128]{4,2,3,0,1:T(8,128)(2,1)S(1)}, bf16[2,1,32,2,128]{4,2,3,0,1:T(8,128)(2,1)S(1)}, u32[]{:S(2)}, u32[]{:S(2)}) collective-permute-start(bf16[2,1,32,2,128]{4,2,3,0,1:T(8,128)(2,1)S(1)} %get-tuple-element.633), channel_id=1, source_target_pairs={{0,24},{2,26},{4,28},{6,30},{8,16},{10,18},{12,20},{14,22},{16,8},... | collective-permute-start | bytes 98312 | tf_op jit(solution)/shard_map/ppermute | solution.py:24
  46.2 5.3 %collective-permute-start.12 = (bf16[2,1,32,2,128]{4,2,3,0,1:T(8,128)(2,1)S(1)}, bf16[2,1,32,2,128]{4,2,3,0,1:T(8,128)(2,1)S(1)}, u32[]{:S(2)}, u32[]{:S(2)}) collective-permute-start(bf16[2,1,32,2,128]{4,2,3,0,1:T(8,128)(2,1)S(1)} %get-tuple-element.632), channel_id=1, source_target_pairs={{0,26},{2,24},{4,30},{6,28},{8,18},{10,16},{12,22},{14,20},{16,10}... | collective-permute-start | bytes 98312 | tf_op jit(solution)/shard_map/ppermute | solution.py:24
  46.4 7.1 %collective-permute-start.13 = (bf16[2,1,32,2,128]{4,2,3,0,1:T(8,128)(2,1)S(1)}, bf16[2,1,32,2,128]{4,2,3,0,1:T(8,128)(2,1)S(1)}, u32[]{:S(2)}, u32[]{:S(2)}) collective-permute-start(bf16[2,1,32,2,128]{4,2,3,0,1:T(8,128)(2,1)S(1)} %get-tuple-element.631), channel_id=1, source_target_pairs={{0,28},{2,30},{4,24},{6,26},{8,20},{10,22},{12,16},{14,18},{16,12}... | collective-permute-start | bytes 98312 | tf_op jit(solution)/shard_map/ppermute | solution.py:24
  50.8 6.1 %collective-permute-start.14 = (bf16[2,1,32,2,128]{4,2,3,0,1:T(8,128)(2,1)S(1)}, bf16[2,1,32,2,128]{4,2,3,0,1:T(8,128)(2,1)S(1)}, u32[]{:S(2)}, u32[]{:S(2)}) collective-permute-start(bf16[2,1,32,2,128]{4,2,3,0,1:T(8,128)(2,1)S(1)} %get-tuple-element.630), channel_id=1, source_target_pairs={{0,30},{2,28},{4,26},{6,24},{8,22},{10,20},{12,18},{14,16},{16,14}... | collective-permute-start | bytes 98312 | tf_op jit(solution)/shard_map/ppermute | solution.py:24
  58.9 30.6 %all-to-all-start.4 = ((bf16[128,32,128]{2,0,1:T(8,128)(2,1)}), bf16[128,32,128]{2,0,1:T(8,128)(2,1)}, u32[]{:S(2)}, u32[]{:S(2)}) async-start(bf16[128,32,128]{2,0,1:T(8,128)(2,1)} %copy.110), calls=%async_computation.4 | async-start | bytes 2097152 | tf_op jit(solution)/shard_map/all_to_all | solution.py:59
  123.8 18.1 %all-to-all-start.5 = ((bf16[256,16,128]{2,1,0:T(8,128)(2,1)}), bf16[256,16,128]{2,1,0:T(8,128)(2,1)S(1)}, u32[]{:S(2)}, u32[]{:S(2)}) async-start(bf16[256,16,128]{2,1,0:T(8,128)(2,1)} %bitcast.106), calls=%async_computation.5 | async-start | bytes 2097152 | tf_op jit(solution)/shard_map/all_to_all | solution.py:190
  141.8 28.3 %copy-start.14 = (bf16[256,16,128]{2,1,0:T(8,128)(2,1)}, bf16[256,16,128]{2,1,0:T(8,128)(2,1)S(1)}, u32[]{:S(2)}) copy-start(bf16[256,16,128]{2,1,0:T(8,128)(2,1)S(1)} %all-to-all-done.5) | copy-start | bytes 3145732
  170.1 19.6 %all-to-all-start.3 = ((bf16[256,16,128]{2,1,0:T(8,128)(2,1)}), bf16[256,16,128]{2,1,0:T(8,128)(2,1)}, u32[]{:S(2)}, u32[]{:S(2)}) async-start(bf16[256,16,128]{2,1,0:T(8,128)(2,1)} %bitcast.318), calls=%async_computation.3 | async-start | bytes 2097152 | tf_op jit(solution)/shard_map/all_to_all | solution.py:189
  189.7 7.8 %all-to-all-start.8 = ((bf16[256,2,128]{2,1,0:T(2,128)(2,1)}), bf16[256,2,128]{2,1,0:T(2,128)(2,1)S(1)}, u32[]{:S(2)}, u32[]{:S(2)}) async-start(bf16[256,2,128]{2,1,0:T(2,128)(2,1)} %copy.138), calls=%async_computation.8 | async-start | bytes 262144 | tf_op jit(solution)/shard_map/all_to_all | solution.py:194
  197.6 7.8 %all-to-all-start.7 = ((bf16[256,2,128]{2,1,0:T(2,128)(2,1)}), bf16[256,2,128]{2,1,0:T(2,128)(2,1)S(1)}, u32[]{:S(2)}, u32[]{:S(2)}) async-start(bf16[256,2,128]{2,1,0:T(2,128)(2,1)} %copy.133), calls=%async_computation.7 | async-start | bytes 262144 | tf_op jit(solution)/shard_map/all_to_all | solution.py:193
  (23 other events, 121.4 us)
